TPU v7x, 128 devices: a whole 4x4x4 slice. The times are simulated.
128 devices in a mesh: body: 2 (over core), sub: 64 (over x, y, z).
Axes of the slice: x: 4, y: 4, z: 4, core: 2. Of those that a mesh axis runs over, the one named last changes fastest.
Arguments:
- rhs: float32 [8, 4096, 256], P(None, 'sub'), may hold values from -50 to 50
- compliance: float32 [4096, 256], P('sub'), may hold values from 0.5 to 2
- plate_owner: int32 [4096, 1], P('sub'), may hold values from 0 to 63; in each aligned block of 64 rows (0 to 63, 64 to 127, ...) at most 2 rows name the same one
- found_owner: int32 [4096, 1], P('sub'), may hold values from 0 to 63; in each aligned block of 64 rows (0 to 63, 64 to 127, ...) at most 2 rows name the same one
- slot_pairs: int32 [4096, 2], P('sub'), may hold values from 0 to 7
- active: int32 [4096], P('sub'), may hold values 0 or 1
- inverse: bfloat16 [2, 64, 2048, 2048], P('body', 'sub'), may hold values from -0.06 to 4, as said below
Outputs:
- multipliers: float32 [8, 4096, 256], P(None, 'sub')
Inputs may be any that keep to these rules, and one draw needn't show every extreme that they name: `plate_owner`: at most 2 patches among the list of one index of sub name the same plate substructure; some list names one exactly 2 times. `found_owner`: at most 2 patches among the list of one index of sub name the same foundation substructure; some list names one exactly 2 times. Each block inverse[b, t] is symmetric positive definite.
All inputs are finite; a program needn't handle non-finite values. No bound on the sum of `active` on one device may be relied on, other than what follows from the above.
Results may differ from a plain program's by a relative error of at most 0.0055.
Values sent between devices are 32-bit elements; how exact they have to be, the bound alone decides.
A program may use at most 64 MiB of HBM per device.

v0:
```python
import jax
import jax.numpy as jnp
from jax import lax
from jax.sharding import PartitionSpec as P

ITERS = 4


def products(left, right):
    return jnp.sum(left * right, axis=(1, 2))


def squares(residual):
    return lax.psum(products(residual, residual), "sub")


def on_device(rhs, compliance, plate_owner, found_owner, slot_pairs, active, inverse):
    nsub = lax.axis_size("sub")
    side = lax.axis_index("body")
    ncase, npatch, block_width = rhs.shape
    local_inverse_block = inverse[0, 0]
    number_of_slots = local_inverse_block.shape[0] // block_width
    room = max(2, 2 * npatch // nsub)
    nrow = nsub * room
    owner = jnp.where(side == 0, plate_owner[:, 0], found_owner[:, 0])
    slot = jnp.where(side == 0, slot_pairs[:, 0], slot_pairs[:, 1])
    patch_index = jnp.arange(npatch, dtype=jnp.int32)
    earlier = patch_index[None, :] < patch_index[:, None]
    same_owner = owner[None, :] == owner[:, None]
    rank = jnp.sum(jnp.where(earlier & same_owner, 1, 0), axis=1).astype(jnp.int32)
    dest_row = owner * room + rank
    placed = dest_row[None, :] == jnp.arange(nrow, dtype=jnp.int32)[:, None]
    source = jnp.sum(jnp.where(placed, patch_index[None, :], 0), axis=1)
    filled = jnp.any(placed, axis=1)
    sent_slot = jnp.where(filled, jnp.take(slot, source), -1)
    received_slot = lax.all_to_all(sent_slot, "sub", split_axis=0, concat_axis=0, tiled=True)
    slot_lookup_table = (
        received_slot[None, :] == jnp.arange(number_of_slots, dtype=jnp.int32)[:, None]
    ).astype(jnp.float32)
    send_valid = filled.astype(jnp.float32)[None, :, None]
    keep = active.astype(jnp.float32)[None, :, None]
    residual = keep * rhs
    solution = jnp.zeros_like(rhs)
    direction = residual
    norm_now = squares(residual)
    for step in range(ITERS):
        outgoing = jnp.take(direction, source, axis=1) * send_valid
        column_entries = lax.all_to_all(outgoing, "sub", split_axis=1, concat_axis=1, tiled=True)
        load_vectors = jnp.einsum(
            "sb,rbk->rsk", slot_lookup_table, column_entries, precision=lax.Precision.HIGHEST
        )
        load_vectors = load_vectors.reshape(
            column_entries.shape[0], number_of_slots * block_width
        ).astype(jnp.bfloat16)
        response = jnp.dot(load_vectors, local_inverse_block, preferred_element_type=jnp.float32)
        plate_piece = lax.all_gather(response[None], "sub", axis=0, tiled=True)
        start = jnp.int32(0)
        slot_count = plate_piece.shape[0]
        local = jnp.clip(owner, 0, slot_count - 1)
        block_list = plate_piece.reshape(
            slot_count, plate_piece.shape[1], number_of_slots, block_width
        )
        chosen = block_list[local, :, slot, :]
        inside = (owner >= start) & (owner < start + slot_count)
        own_part = jnp.transpose(jnp.where(inside[:, None, None], chosen, 0.0), (1, 0, 2))
        total = lax.psum(own_part, "body")
        image = keep * (total + compliance[None] * direction)
        alpha = norm_now / lax.psum(products(direction, image), "sub")
        solution = solution + alpha[:, None, None] * direction
        residual = residual - alpha[:, None, None] * image
        norm_next = squares(residual)
        direction = residual + (norm_next / norm_now)[:, None, None] * direction
        norm_now = norm_next
    return solution


def solution(mesh):
    in_specs = (
        P(None, "sub", None),
        P("sub", None),
        P("sub", None),
        P("sub", None),
        P("sub", None),
        P("sub"),
        P("body", "sub", None, None),
    )
    out_specs = P(None, "sub", None)
    return jax.shard_map(
        on_device, mesh=mesh, in_specs=in_specs, out_specs=out_specs, check_vma=False
    )
```

profile of v0, /device:TPU:0, one launch (start us, length us, event | category | flops | bytes accessed | tf_op | source)
XLA Modules:
  0.0 1756.6 jit_solution(2245857336711810583)
XLA Ops:
  10.7 11.5 all-to-all-start.1
  26.3 5.3 all-to-all-done.1
  38.1 16.5 all-to-all-done
  55.4 5.3 fusion.6
  60.8 65.0 %all-gather.9.cloned.1.call-done = f32[512,2048]{1,0:T(8,128)} async-done(((f32[8,2048]{1,0:T(8,128)}), f32[512,2048]{1,0:T(8,128)}) %all-gather.9.cloned.1.call-update) | async-done | bytes 4194320 | tf_op jit(solution)/shard_map/all_gather | solution.py:56
  129.6 21.8 %all-reduce.6.cloned.1.call-done = f32[8,64,256]{2,0,1:T(8,128)} async-done(((f32[8,64,256]{2,0,1:T(8,128)}), f32[8,64,256]{2,0,1:T(8,128)}) %all-reduce.6.cloned.1.call-update) | async-done | bytes 524304 | tf_op jit(solution)/shard_map/psum | solution.py:66
  153.1 179.1 %all-reduce = (f32[8]{0:T(128)S(1)}, f32[8]{0:T(128)S(1)}) all-reduce(f32[8]{0:T(128)S(1)} %get-tuple-element.7, f32[8]{0:T(128)S(1)} %get-tuple-element.6), channel_id=1, replica_groups=mesh['body'=2,'sub'=64] {'sub'}, use_global_device_ids=true, to_apply=%region_1.2 | all-reduce | flops 16 | bytes 128 | tf_op jit(solution)/shard_map/psum | solution.py:14
  333.8 172.0 %psum.87 = f32[8]{0:T(128)S(1)} all-reduce(f32[8]{0:T(128)S(1)} %multiply_reduce_fusion.5), channel_id=1, replica_groups=mesh['body'=2,'sub'=64] {'sub'}, use_global_device_ids=true, to_apply=%region_9.11 | all-reduce | flops 8 | bytes 64 | tf_op jit(solution)/shard_map/psum | solution.py:14
  508.3 18.7 %all_to_all.26 = f32[8,128,256]{2,0,1:T(8,128)S(1)} all-to-all(f32[8,128,256]{2,0,1:T(8,128)S(1)} %bitcast_multiply_fusion.2), channel_id=1, replica_groups=mesh['body'=2,'sub'=64] {'sub'}, dimensions={1} | all-to-all | bytes 2097152 | tf_op jit(solution)/shard_map/all_to_all | solution.py:48
  527.8 5.3 fusion.4
  533.1 64.8 %all-gather.11.cloned.1.call-done = f32[512,2048]{1,0:T(8,128)} async-done(((f32[8,2048]{1,0:T(8,128)}), f32[512,2048]{1,0:T(8,128)}) %all-gather.11.cloned.1.call-update) | async-done | bytes 4194320 | tf_op jit(solution)/shard_map/all_gather | solution.py:56
  601.8 21.8 %all-reduce.8.cloned.1.call-done = f32[8,64,256]{2,0,1:T(8,128)} async-done(((f32[8,64,256]{2,0,1:T(8,128)}), f32[8,64,256]{2,0,1:T(8,128)}) %all-reduce.8.cloned.1.call-update) | async-done | bytes 524304 | tf_op jit(solution)/shard_map/psum | solution.py:66
  624.9 179.2 %psum.89 = f32[8]{0:T(128)S(1)} all-reduce(f32[8]{0:T(128)S(1)} %multiply_reduce_fusion.4), channel_id=1, replica_groups=mesh['body'=2,'sub'=64] {'sub'}, use_global_device_ids=true, to_apply=%region_12.14 | all-reduce | flops 8 | bytes 64 | tf_op jit(solution)/shard_map/psum | solution.py:68
  805.8 171.8 %psum.90 = f32[8]{0:T(128)S(1)} all-reduce(f32[8]{0:T(128)S(1)} %get-tuple-element.10), channel_id=1, replica_groups=mesh['body'=2,'sub'=64] {'sub'}, use_global_device_ids=true, to_apply=%region_14.16 | all-reduce | flops 8 | bytes 64 | tf_op jit(solution)/shard_map/psum | solution.py:14
  978.9 18.5 %all_to_all.27 = f32[8,128,256]{2,0,1:T(8,128)S(1)} all-to-all(f32[8,128,256]{2,0,1:T(8,128)S(1)} %bitcast_multiply_fusion.1), channel_id=1, replica_groups=mesh['body'=2,'sub'=64] {'sub'}, dimensions={1} | all-to-all | bytes 2097152 | tf_op jit(solution)/shard_map/all_to_all | solution.py:48
  1003.4 64.8 %all-gather.13.cloned.1.call-done = f32[512,2048]{1,0:T(8,128)} async-done(((f32[8,2048]{1,0:T(8,128)}), f32[512,2048]{1,0:T(8,128)}) %all-gather.13.cloned.1.call-update) | async-done | bytes 4194320 | tf_op jit(solution)/shard_map/all_gather | solution.py:56
  1072.0 21.8 %all-reduce.10.cloned.1.call-done = f32[8,64,256]{2,0,1:T(8,128)} async-done(((f32[8,64,256]{2,0,1:T(8,128)}), f32[8,64,256]{2,0,1:T(8,128)}) %all-reduce.10.cloned.1.call-update) | async-done | bytes 524304 | tf_op jit(solution)/shard_map/psum | solution.py:66
  1095.2 179.1 %psum.92 = f32[8]{0:T(128)S(1)} all-reduce(f32[8]{0:T(128)S(1)} %multiply_reduce_fusion.2), channel_id=1, replica_groups=mesh['body'=2,'sub'=64] {'sub'}, use_global_device_ids=true, to_apply=%region_17.19 | all-reduce | flops 8 | bytes 64 | tf_op jit(solution)/shard_map/psum | solution.py:68
  1275.7 172.6 %psum.93 = f32[8]{0:T(128)S(1)} all-reduce(f32[8]{0:T(128)S(1)} %multiply_reduce_fusion.1), channel_id=1, replica_groups=mesh['body'=2,'sub'=64] {'sub'}, use_global_device_ids=true, to_apply=%region_19.21 | all-reduce | flops 8 | bytes 64 | tf_op jit(solution)/shard_map/psum | solution.py:14
  1452.8 18.7 %all_to_all.28 = f32[8,128,256]{2,0,1:T(8,128)S(1)} all-to-all(f32[8,128,256]{2,0,1:T(8,128)S(1)} %bitcast_multiply_fusion), channel_id=1, replica_groups=mesh['body'=2,'sub'=64] {'sub'}, dimensions={1} | all-to-all | bytes 2097152 | tf_op jit(solution)/shard_map/all_to_all | solution.py:48
  1472.3 5.2 fusion
  1477.5 64.8 %all-gather.15.cloned.1.call-done = f32[512,2048]{1,0:T(8,128)} async-done(((f32[8,2048]{1,0:T(8,128)}), f32[512,2048]{1,0:T(8,128)}) %all-gather.15.cloned.1.call-update) | async-done | bytes 4194320 | tf_op jit(solution)/shard_map/all_gather | solution.py:56
  1546.2 21.9 %all-reduce.12.cloned.1.call-done = f32[8,64,256]{2,0,1:T(8,128)} async-done(((f32[8,64,256]{2,0,1:T(8,128)}), f32[8,64,256]{2,0,1:T(8,128)}) %all-reduce.12.cloned.1.call-update) | async-done | bytes 524304 | tf_op jit(solution)/shard_map/psum | solution.py:66
  1569.4 179.1 %psum.95 = f32[8]{0:T(128)S(1)} all-reduce(f32[8]{0:T(128)S(1)} %multiply_reduce_fusion), channel_id=1, replica_groups=mesh['body'=2,'sub'=64] {'sub'}, use_global_device_ids=true, to_apply=%region_22.24 | all-reduce | flops 8 | bytes 64 | tf_op jit(solution)/shard_map/psum | solution.py:68
  (89 shorter events, 58.5 us)
Async XLA Ops:
  10.7 21.0 %all-to-all-start.1 = ((s32[64,2,1]{1,2,0:T(1,128)}), s32[64,2,1]{1,2,0:T(1,128)S(1)}, u32[]{:S(2)}, u32[]{:S(2)}) async-start(s32[64,2,1]{1,2,0:T(1,128)} %bitcast.5), calls=%async_computation.1 | async-start | bytes 65536 | tf_op jit(solution)/shard_map/all_to_all | solution.py:36
  31.7 23.0 %all-to-all-start = ((f32[8,128,256]{2,0,1:T(8,128)}), f32[8,128,256]{2,0,1:T(8,128)S(1)}, u32[]{:S(2)}, u32[]{:S(2)}) async-start(f32[8,128,256]{2,0,1:T(8,128)} %bitcast_multiply_fusion.3), calls=%async_computation | async-start | bytes 2097152 | tf_op jit(solution)/shard_map/all_to_all | solution.py:48
  36.7 89.1 %all-gather.9.cloned.1.call-start = ((), (), s32[]{:S(2)}) async-start(), calls=%async_computation.9 | async-start | bytes 4259840 | tf_op jit(solution)/shard_map/all_gather | solution.py:56
  55.4 96.1 %copy-start = (f32[8,64,256]{2,1,0:T(8,128)S(1)}, f32[8,64,256]{2,1,0:T(8,128)}, u32[]{:S(2)}) copy-start(f32[8,64,256]{2,1,0:T(8,128)} %param.9) | copy-start | bytes 1572868
  55.4 96.1 %copy-start.2 = (f32[64,256]{1,0:T(8,128)S(1)}, f32[64,256]{1,0:T(8,128)}, u32[]{:S(2)}) copy-start(f32[64,256]{1,0:T(8,128)} %param.10) | copy-start | bytes 196612
  60.7 90.7 %all-reduce.6.cloned.1.call-start = ((), (), s32[]{:S(2)}) async-start(), calls=%async_computation.5 | async-start | bytes 1048576 | tf_op jit(solution)/shard_map/psum | solution.py:66
  129.6 468.3 %all-gather.11.cloned.1.call-start = ((), (), s32[]{:S(2)}) async-start(), calls=%async_computation.10 | async-start | bytes 4259840 | tf_op jit(solution)/shard_map/all_gather | solution.py:56
  527.7 276.4 %copy-start.1 = (f32[8,64,256]{2,0,1:T(8,128)S(1)}, f32[8,64,256]{2,0,1:T(8,128)}, u32[]{:S(2)}) copy-start(f32[8,64,256]{2,0,1:T(8,128)} %all-reduce.6.cloned.1.call-done) | copy-start | bytes 1572868
  533.0 90.5 %all-reduce.8.cloned.1.call-start = ((), (), s32[]{:S(2)}) async-start(), calls=%async_computation.6 | async-start | bytes 1048576 | tf_op jit(solution)/shard_map/psum | solution.py:66
  601.7 466.4 %all-gather.13.cloned.1.call-start = ((), (), s32[]{:S(2)}) async-start(), calls=%async_computation.11 | async-start | bytes 4259840 | tf_op jit(solution)/shard_map/all_gather | solution.py:56
  1003.3 90.5 %all-reduce.10.cloned.1.call-start = ((), (), s32[]{:S(2)}) async-start(), calls=%async_computation.7 | async-start | bytes 1048576 | tf_op jit(solution)/shard_map/psum | solution.py:66
  1072.0 470.3 %all-gather.15.cloned.1.call-start = ((), (), s32[]{:S(2)}) async-start(), calls=%async_computation.12 | async-start | bytes 4259840 | tf_op jit(solution)/shard_map/all_gather | solution.py:56
  1477.5 90.5 %all-reduce.12.cloned.1.call-start = ((), (), s32[]{:S(2)}) async-start(), calls=%async_computation.8 | async-start | bytes 1048576 | tf_op jit(solution)/shard_map/psum | solution.py:66
Sparse Core Ops, SparseCore 0:
  60.8 64.8 all-gather.8
  129.7 21.7 all-reduce.5
  533.2 64.6 all-gather.10
  601.8 21.6 all-reduce.7
  1003.4 64.6 all-gather.12
  1072.1 21.7 all-reduce.9
  1477.6 64.6 all-gather.14
  1546.3 21.6 all-reduce.11
where the time goes:
time: 1760 us
  blocking collectives  1290 us (73%)
  waiting for transfers between devices  369 us (21%)
  other arithmetic  26.1 us (1%)
  matrix products  23.8 us (1%)
  local copies, waits for them, and re-layouts  18.8 us (1%)
    psum x4, blocking collectives, squares(): return lax.psum(products(residual, residual), 'sub')  695 us
    psum x3, blocking collectives, on_device(): alpha = norm_now / lax.psum(products(direction, image), 'sub')  537 us
    all_gather x4, waiting for transfers between devices, on_device(): plate_piece = lax.all_gather(response[None], 'sub', axis=0, tiled=True)  259 us
    psum x4, waiting for transfers between devices, on_device(): total = lax.psum(own_part, 'body')  87.3 us
    all_to_all x3, blocking collectives, on_device(): lax.all_to_all(outgoing, 'sub', split_axis=1, concat_axis=1, tiled=True)  55.9 us
  transfers between devices with their start and end apart: 10, of which 10 were waited for; matrix products, arithmetic and copies ran while one was open for 0% of the time, Pallas kernels for 0%

commit v1 on v0

--- a/solution.py
+++ b/solution.py
@@ -53,7 +53,9 @@
             column_entries.shape[0], number_of_slots * block_width
         ).astype(jnp.bfloat16)
         response = jnp.dot(load_vectors, local_inverse_block, preferred_element_type=jnp.float32)
-        plate_piece = lax.all_gather(response[None], "sub", axis=0, tiled=True)
+        plate_piece = jnp.concatenate(
+            lax.all_to_all(jnp.stack([response[None]] * lax.axis_size("sub")), "sub", 0, 0), axis=0
+        )
         start = jnp.int32(0)
         slot_count = plate_piece.shape[0]
         local = jnp.clip(owner, 0, slot_count - 1)

time: 1760 us -> 1680 us (0.955)
  waiting for transfers between devices: 369 us -> 105 us
  blocking collectives: 1290 us -> 1470 us
    all_gather x4 -> x0, waiting for transfers between devices: 259 us -> none  [on_device(): plate_piece = lax.all_gather(response[None], 'sub', axis=0, tiled=True)]
    all_to_all x0 -> x4, blocking collectives: none -> 163 us  [on_device(): lax.all_to_all(jnp.stack([response[None]] * lax.axis_size('sub')), 'sub',...]
  transfers between devices with their start and end apart: 10 -> 6, of which waited for: 10 -> 6; matrix products, arithmetic and copies ran while one was open for 0% -> 0% of each run, Pallas kernels for 0% -> 0%
where the time goes in v1:
time: 1680 us
  blocking collectives  1470 us (88%)
  waiting for transfers between devices  105 us (6%)
  other arithmetic  27.3 us (2%)
  local copies, waits for them, and re-layouts  21.8 us (1%)
  matrix products  21.2 us (1%)
    psum x4, blocking collectives, squares(): return lax.psum(products(residual, residual), 'sub')  706 us
    psum x3, blocking collectives, on_device(): alpha = norm_now / lax.psum(products(direction, image), 'sub')  537 us
    all_to_all x4, blocking collectives, on_device(): lax.all_to_all(jnp.stack([response[None]] * lax.axis_size('sub')), 'sub',...  163 us
    psum x4, waiting for transfers between devices, on_device(): total = lax.psum(own_part, 'body')  82.7 us
    all_to_all x3, blocking collectives, on_device(): lax.all_to_all(outgoing, 'sub', split_axis=1, concat_axis=1, tiled=True)  65.5 us
  transfers between devices with their start and end apart: 6, of which 6 were waited for; matrix products, arithmetic and copies ran while one was open for 0% of the time, Pallas kernels for 0%

profile of v1, /device:TPU:0, one launch (start us, length us, event | category | flops | bytes accessed | tf_op | source)
XLA Modules:
  0.0 1676.6 jit_solution(2410707879900401876)
XLA Ops:
  10.7 11.5 all-to-all-start.1
  26.3 5.3 all-to-all-done.1
  31.7 5.0 all-to-all-start
  38.1 16.5 all-to-all-done
  55.4 4.6 fusion.6
  60.5 55.9 %all_to_all.46 = f32[64,1,8,2048]{3,2,1,0:T(8,128)} all-to-all(f32[64,1,8,2048]{3,2,1,0:T(8,128)S(1)} %stack.12), channel_id=1, replica_groups=mesh['body'=2,'sub'=64] {'sub'}, dimensions={0} | all-to-all | bytes 8388608 | tf_op jit(solution)/shard_map/all_to_all | solution.py:57
  120.3 21.3 %all-reduce.6.cloned.1.call-done = f32[8,64,256]{2,0,1:T(8,128)} async-done(((f32[8,64,256]{2,0,1:T(8,128)}), f32[8,64,256]{2,0,1:T(8,128)}) %all-reduce.6.cloned.1.call-update) | async-done | bytes 524304 | tf_op jit(solution)/shard_map/psum | solution.py:68
  143.2 179.1 %all-reduce = (f32[8]{0:T(128)S(1)}, f32[8]{0:T(128)S(1)}) all-reduce(f32[8]{0:T(128)S(1)} %get-tuple-element.7, f32[8]{0:T(128)S(1)} %get-tuple-element.6), channel_id=1, replica_groups=mesh['body'=2,'sub'=64] {'sub'}, use_global_device_ids=true, to_apply=%region_1.2 | all-reduce | flops 16 | bytes 128 | tf_op jit(solution)/shard_map/psum | solution.py:14
  323.9 174.9 %psum.87 = f32[8]{0:T(128)S(1)} all-reduce(f32[8]{0:T(128)S(1)} %multiply_reduce_fusion.5), channel_id=1, replica_groups=mesh['body'=2,'sub'=64] {'sub'}, use_global_device_ids=true, to_apply=%region_9.11 | all-reduce | flops 8 | bytes 64 | tf_op jit(solution)/shard_map/psum | solution.py:14
  501.3 21.7 %all_to_all.47 = f32[8,128,256]{2,0,1:T(8,128)S(1)} all-to-all(f32[8,128,256]{2,0,1:T(8,128)S(1)} %bitcast_multiply_fusion.2), channel_id=1, replica_groups=mesh['body'=2,'sub'=64] {'sub'}, dimensions={1} | all-to-all | bytes 2097152 | tf_op jit(solution)/shard_map/all_to_all | solution.py:48
  528.8 35.7 %all_to_all.48 = f32[64,1,8,2048]{3,2,1,0:T(8,128)} all-to-all(f32[64,1,8,2048]{3,2,1,0:T(8,128)S(1)} %stack.13), channel_id=1, replica_groups=mesh['body'=2,'sub'=64] {'sub'}, dimensions={0} | all-to-all | bytes 8388608 | tf_op jit(solution)/shard_map/all_to_all | solution.py:57
  568.4 20.5 %all-reduce.8.cloned.1.call-done = f32[8,64,256]{2,0,1:T(8,128)} async-done(((f32[8,64,256]{2,0,1:T(8,128)}), f32[8,64,256]{2,0,1:T(8,128)}) %all-reduce.8.cloned.1.call-update) | async-done | bytes 524304 | tf_op jit(solution)/shard_map/psum | solution.py:68
  590.2 179.1 %psum.89 = f32[8]{0:T(128)S(1)} all-reduce(f32[8]{0:T(128)S(1)} %multiply_reduce_fusion.4), channel_id=1, replica_groups=mesh['body'=2,'sub'=64] {'sub'}, use_global_device_ids=true, to_apply=%region_12.14 | all-reduce | flops 8 | bytes 64 | tf_op jit(solution)/shard_map/psum | solution.py:70
  771.0 175.8 %psum.90 = f32[8]{0:T(128)S(1)} all-reduce(f32[8]{0:T(128)S(1)} %get-tuple-element.10), channel_id=1, replica_groups=mesh['body'=2,'sub'=64] {'sub'}, use_global_device_ids=true, to_apply=%region_14.16 | all-reduce | flops 8 | bytes 64 | tf_op jit(solution)/shard_map/psum | solution.py:14
  950.2 21.7 %all_to_all.49 = f32[8,128,256]{2,0,1:T(8,128)S(1)} all-to-all(f32[8,128,256]{2,0,1:T(8,128)S(1)} %bitcast_multiply_fusion.1), channel_id=1, replica_groups=mesh['body'=2,'sub'=64] {'sub'}, dimensions={1} | all-to-all | bytes 2097152 | tf_op jit(solution)/shard_map/all_to_all | solution.py:48
  972.6 4.6 fusion.2
  977.7 35.7 %all_to_all.50 = f32[64,1,8,2048]{3,2,1,0:T(8,128)} all-to-all(f32[64,1,8,2048]{3,2,1,0:T(8,128)S(1)} %stack.14), channel_id=1, replica_groups=mesh['body'=2,'sub'=64] {'sub'}, dimensions={0} | all-to-all | bytes 8388608 | tf_op jit(solution)/shard_map/all_to_all | solution.py:57
  1017.3 20.5 %all-reduce.10.cloned.1.call-done = f32[8,64,256]{2,0,1:T(8,128)} async-done(((f32[8,64,256]{2,0,1:T(8,128)}), f32[8,64,256]{2,0,1:T(8,128)}) %all-reduce.10.cloned.1.call-update) | async-done | bytes 524304 | tf_op jit(solution)/shard_map/psum | solution.py:68
  1039.1 179.1 %psum.92 = f32[8]{0:T(128)S(1)} all-reduce(f32[8]{0:T(128)S(1)} %multiply_reduce_fusion.2), channel_id=1, replica_groups=mesh['body'=2,'sub'=64] {'sub'}, use_global_device_ids=true, to_apply=%region_17.19 | all-reduce | flops 8 | bytes 64 | tf_op jit(solution)/shard_map/psum | solution.py:70
  1219.6 176.1 %psum.93 = f32[8]{0:T(128)S(1)} all-reduce(f32[8]{0:T(128)S(1)} %multiply_reduce_fusion.1), channel_id=1, replica_groups=mesh['body'=2,'sub'=64] {'sub'}, use_global_device_ids=true, to_apply=%region_19.21 | all-reduce | flops 8 | bytes 64 | tf_op jit(solution)/shard_map/psum | solution.py:14
  1400.3 22.2 %all_to_all.51 = f32[8,128,256]{2,0,1:T(8,128)S(1)} all-to-all(f32[8,128,256]{2,0,1:T(8,128)S(1)} %bitcast_multiply_fusion), channel_id=1, replica_groups=mesh['body'=2,'sub'=64] {'sub'}, dimensions={1} | all-to-all | bytes 2097152 | tf_op jit(solution)/shard_map/all_to_all | solution.py:48
  1428.2 35.7 %all_to_all.52 = f32[64,1,8,2048]{3,2,1,0:T(8,128)} all-to-all(f32[64,1,8,2048]{3,2,1,0:T(8,128)S(1)} %stack.15), channel_id=1, replica_groups=mesh['body'=2,'sub'=64] {'sub'}, dimensions={0} | all-to-all | bytes 8388608 | tf_op jit(solution)/shard_map/all_to_all | solution.py:57
  1467.8 20.5 %all-reduce.12.cloned.1.call-done = f32[8,64,256]{2,0,1:T(8,128)} async-done(((f32[8,64,256]{2,0,1:T(8,128)}), f32[8,64,256]{2,0,1:T(8,128)}) %all-reduce.12.cloned.1.call-update) | async-done | bytes 524304 | tf_op jit(solution)/shard_map/psum | solution.py:68
  1489.6 179.1 %psum.95 = f32[8]{0:T(128)S(1)} all-reduce(f32[8]{0:T(128)S(1)} %multiply_reduce_fusion), channel_id=1, replica_groups=mesh['body'=2,'sub'=64] {'sub'}, use_global_device_ids=true, to_apply=%region_22.24 | all-reduce | flops 8 | bytes 64 | tf_op jit(solution)/shard_map/psum | solution.py:70
  (85 shorter events, 61.4 us)
Async XLA Ops:
  10.7 21.0 %all-to-all-start.1 = ((s32[64,2,1]{1,2,0:T(1,128)}), s32[64,2,1]{1,2,0:T(1,128)S(1)}, u32[]{:S(2)}, u32[]{:S(2)}) async-start(s32[64,2,1]{1,2,0:T(1,128)} %bitcast.5), calls=%async_computation.1 | async-start | bytes 65536 | tf_op jit(solution)/shard_map/all_to_all | solution.py:36
  31.7 23.0 %all-to-all-start = ((f32[8,128,256]{2,0,1:T(8,128)}), f32[8,128,256]{2,0,1:T(8,128)S(1)}, u32[]{:S(2)}, u32[]{:S(2)}) async-start(f32[8,128,256]{2,0,1:T(8,128)} %bitcast_multiply_fusion.3), calls=%async_computation | async-start | bytes 2097152 | tf_op jit(solution)/shard_map/all_to_all | solution.py:48
  36.7 104.8 %all-reduce.6.cloned.1.call-start = ((), (), s32[]{:S(2)}) async-start(), calls=%async_computation.9 | async-start | bytes 1048576 | tf_op jit(solution)/shard_map/psum | solution.py:68
  60.0 81.6 %copy-start = (f32[8,64,256]{2,1,0:T(8,128)S(1)}, f32[8,64,256]{2,1,0:T(8,128)}, u32[]{:S(2)}) copy-start(f32[8,64,256]{2,1,0:T(8,128)} %param.9) | copy-start | bytes 1572868
  60.0 81.6 %copy-start.2 = (f32[64,256]{1,0:T(8,128)S(1)}, f32[64,256]{1,0:T(8,128)}, u32[]{:S(2)}) copy-start(f32[64,256]{1,0:T(8,128)} %param.10) | copy-start | bytes 196612
  120.2 468.6 %all-reduce.8.cloned.1.call-start = ((), (), s32[]{:S(2)}) async-start(), calls=%async_computation.10 | async-start | bytes 1048576 | tf_op jit(solution)/shard_map/psum | solution.py:68
  528.3 241.0 %copy-start.1 = (f32[8,64,256]{2,0,1:T(8,128)S(1)}, f32[8,64,256]{2,0,1:T(8,128)}, u32[]{:S(2)}) copy-start(f32[8,64,256]{2,0,1:T(8,128)} %all-reduce.6.cloned.1.call-done) | copy-start | bytes 1572868
  568.3 469.4 %all-reduce.10.cloned.1.call-start = ((), (), s32[]{:S(2)}) async-start(), calls=%async_computation.11 | async-start | bytes 1048576 | tf_op jit(solution)/shard_map/psum | solution.py:68
  1017.2 471.0 %all-reduce.12.cloned.1.call-start = ((), (), s32[]{:S(2)}) async-start(), calls=%async_computation.12 | async-start | bytes 1048576 | tf_op jit(solution)/shard_map/psum | solution.py:68
Sparse Core Ops, SparseCore 0:
  120.3 21.1 all-reduce.5
  568.5 20.3 all-reduce.7
  1017.4 20.3 all-reduce.9
  1467.9 20.3 all-reduce.11
